TPU v7x, 32 devices: a whole 2x2x4 slice. The times are simulated.
32 devices in a mesh: dp: 4 (over z), expert: 8 (over y, x, core).
Axes of the slice: x: 2, y: 2, z: 4, core: 2. Of those that a mesh axis runs over, the one named last changes fastest.
Arguments:
- tokens: bfloat16 [256, 3584], P(('dp', 'expert')), may hold values from -6 to 6
- routes: int32 [256, 8], P(('dp', 'expert')), may hold values from 0 to 63, as said below
- gate_values: bfloat16 [256, 8], P(('dp', 'expert')), may hold values from 0.099609375 to 0.5
- expert_map: int32 [64], replicated, may hold values from 0 to 63, as said below
- row_counts: int32 [32], P(('dp', 'expert')), may hold values from 1 to 8, 224 in all
- gate_weight: bfloat16 [8, 3584, 2048], P('expert', None, 'dp'), may hold values from -0.09375 to 0.09375
- up_weight: bfloat16 [8, 3584, 2048], P('expert', None, 'dp'), may hold values from -0.09375 to 0.09375
- down_weight: bfloat16 [8, 2048, 3584], P('expert', 'dp'), may hold values from -0.125 to 0.125
- delta_in: bfloat16 [8, 8, 3584, 256], P('expert', 'dp'), may hold values from -0.09375 to 0.09375
- delta_out: bfloat16 [8, 8, 256, 3584], P('expert', 'dp'), may hold values from -0.375 to 0.375
Outputs:
- mixed: bfloat16 [256, 3584], P(('dp', 'expert'))
Inputs may be any that keep to these rules, and one draw needn't show every extreme that they name: `routes`: each row names 8 different experts, two in each of 4 different bases; at most 8 rows of one device route to one base, and some device has a base that 8 of its rows route to. `expert_map`: A permutation of the 64 slots.
All inputs are finite; a program needn't handle non-finite values. No bound on the sum of `row_counts` on one device may be relied on, other than what follows from the above.
Results may differ from a plain program's by a relative error of at most 0.015.
Values may be sent and summed in bfloat16 or wider, within the bound.
No kernel may reach another device: no remote copies, remote signals or barrier semaphores. Data moves between devices by JAX's collectives and lax.ppermute only.
A program may use at most 64 MiB of HBM per device.

v0:
```python
import jax
import jax.numpy as jnp
from jax import lax
from jax.sharding import PartitionSpec as P

JSLOT = 8
BTOP = 4


def slot_table(routes, gate_values, expert_map, live_mask):
    experts = expert_map.shape[0]
    identity_ids = jnp.arange(experts, dtype=jnp.int32)
    matches = routes[:, :, None] == identity_ids[None, None, :]
    slot_ids = jnp.sum(jnp.where(matches, expert_map[None, None, :], 0), axis=2)
    chosen = slot_ids[:, :, None] == identity_ids[None, None, :]
    spread = jnp.sum(
        jnp.where(chosen, gate_values.astype(jnp.float32)[:, :, None], jnp.float32(0.0)), axis=1
    )
    spread = jnp.where(live_mask[:, None], spread, jnp.float32(0.0))
    return spread.astype(jnp.bfloat16)


def placement_table(slot_gates, base_count, capacity):
    blocks, row_total, slot_count = slot_gates.shape
    grouped = slot_gates.reshape(blocks, row_total, base_count, slot_count // base_count)
    member = jnp.sum((grouped > 0).astype(jnp.int32), axis=3) > 0
    counted = member.astype(jnp.int32)
    before = jnp.cumsum(counted, axis=1) - counted
    target = jnp.where(member, before, -1)
    return (target[:, :, :, None] == jnp.arange(capacity, dtype=jnp.int32)).astype(jnp.bfloat16)


def slice_term(sent_rows, sent_gates, gate_part, up_part, down_part, in_part, out_part, first_slot):
    slot_span = in_part.shape[0]
    gate_value = jnp.dot(sent_rows, gate_part, preferred_element_type=jnp.float32)
    up_value = jnp.dot(sent_rows, up_part, preferred_element_type=jnp.float32)
    hidden = (jax.nn.silu(gate_value) * up_value).astype(jnp.bfloat16)
    shared = jnp.dot(hidden, down_part, preferred_element_type=jnp.float32)
    gate_total = jnp.sum(sent_gates.astype(jnp.float32), axis=1, keepdims=True)
    own_gates = lax.dynamic_slice_in_dim(sent_gates, first_slot, slot_span, 1).astype(jnp.float32)
    latent = jnp.einsum(
        "nd,jdr->jnr", sent_rows, in_part, preferred_element_type=jnp.float32
    ).astype(jnp.bfloat16)
    lifted = jnp.einsum("jnr,jrd->jnd", latent, out_part, preferred_element_type=jnp.float32)
    deltas = jnp.einsum("nj,jnd->nd", own_gates, lifted)
    return gate_total * shared + deltas


def body(
    tokens,
    routes,
    gate_values,
    expert_map,
    row_counts,
    gate_weight,
    up_weight,
    down_weight,
    delta_in,
    delta_out,
):
    row_total = tokens.shape[0]
    width = tokens.shape[1]
    dp_size = lax.axis_size("dp")
    expert_size = lax.axis_size("expert")
    slot_count = expert_map.shape[0]
    capacity = 2 * BTOP * row_total // expert_size
    live_mask = jnp.arange(row_total, dtype=jnp.int32) < row_counts[0]
    slot_gates = slot_table(routes, gate_values, expert_map, live_mask)
    own_placed = placement_table(slot_gates[None], expert_size, capacity)[0]
    all_tokens, all_gates = (
        lax.all_gather(tokens, "dp", axis=0, tiled=True),
        lax.all_gather(slot_gates, "dp", axis=0, tiled=True),
    )
    placed = placement_table(
        all_gates.reshape(dp_size, row_total, slot_count), expert_size, capacity
    )
    sent_rows = jnp.einsum(
        "nrbc,nrd->nbcd",
        placed,
        all_tokens.reshape(dp_size, row_total, width),
        preferred_element_type=jnp.float32,
    ).astype(jnp.bfloat16)
    sent_gates = jnp.einsum(
        "nrbc,nrbj->nbcj",
        placed,
        all_gates.reshape(dp_size, row_total, expert_size, JSLOT),
        preferred_element_type=jnp.float32,
    ).astype(jnp.bfloat16)
    got_rows, got_gates = (
        lax.all_to_all(sent_rows, "expert", split_axis=1, concat_axis=1, tiled=True),
        lax.all_to_all(sent_gates, "expert", split_axis=1, concat_axis=1, tiled=True),
    )
    flat_rows = got_rows.reshape(-1, width)
    flat_gates = got_gates.reshape(-1, JSLOT)
    slot_span = JSLOT // dp_size
    first_slot = lax.axis_index("dp") * slot_span
    gate_part = gate_weight[0]
    up_part = up_weight[0]
    down_part = down_weight[0]
    in_part = delta_in[0]
    out_part = delta_out[0]
    summed = lax.psum_scatter(
        slice_term(
            flat_rows, flat_gates, gate_part, up_part, down_part, in_part, out_part, first_slot
        ).astype(jnp.bfloat16),
        "dp",
        scatter_dimension=0,
        tiled=True,
    )
    results = lax.all_to_all(
        summed.reshape(expert_size, capacity, width),
        "expert",
        split_axis=0,
        concat_axis=0,
        tiled=True,
    )
    mixed = jnp.einsum("rbc,bcd->rd", own_placed, results, preferred_element_type=jnp.float32)
    return mixed.astype(jnp.bfloat16)


def solution(mesh):
    in_specs = (
        P(("dp", "expert"), None),
        P(("dp", "expert"), None),
        P(("dp", "expert"), None),
        P(),
        P(("dp", "expert")),
        P("expert", None, "dp"),
        P("expert", None, "dp"),
        P("expert", "dp", None),
        P("expert", "dp", None, None),
        P("expert", "dp", None, None),
    )
    out_specs = P(("dp", "expert"), None)
    return jax.shard_map(body, mesh=mesh, in_specs=in_specs, out_specs=out_specs, check_vma=False)
```

profile of v0, /device:TPU:0, one launch (start us, length us, event | category | flops | bytes accessed | tf_op | source)
XLA Modules:
  0.0 162.9 jit_solution(12481493179372716351)
XLA Ops:
  6.5 0.7 convert_element_type.85
  7.9 1.0 select_reduce_fusion.1
  8.9 0.1 select_reduce_fusion
  9.0 0.1 select_convert_fusion.1
  9.0 13.6 %all_gather.6 = bf16[32,64]{1,0:T(8,128)(2,1)S(1)} all-gather(bf16[8,64]{1,0:T(8,128)(2,1)S(1)} %select_convert_fusion.1), channel_id=1, replica_groups=mesh['dp'=4,'expert'=8] {'dp'}, dimensions={0}, use_global_device_ids=true | all-gather | bytes 5120 | tf_op jit(solution)/shard_map/all_gather | solution.py:72
  22.7 0.1 reshape_reshape.3
  22.8 0.6 convert_reduce_fusion.1
  23.5 0.1 copy.41
  23.5 0.2 convolution_convert_fusion.1
  23.7 0.7 reshape.106
  24.4 3.7 %all-to-all-start = ((bf16[8,2,128]{2,1,0:T(2,128)(2,1)}), bf16[8,2,128]{2,1,0:T(2,128)(2,1)S(1)}, u32[]{:S(2)}, u32[]{:S(2)}) async-start(bf16[8,2,128]{2,1,0:T(2,128)(2,1)} %reshape.106), calls=%async_computation | async-start | bytes 8192 | tf_op jit(solution)/shard_map/all_to_all | solution.py:91
  28.1 14.0 %all_gather.7 = bf16[32,3584]{1,0:T(8,128)(2,1)S(1)} all-gather(bf16[8,3584]{1,0:T(8,128)(2,1)} %param.10), channel_id=1, replica_groups=mesh['dp'=4,'expert'=8] {'dp'}, dimensions={0}, use_global_device_ids=true | all-gather | bytes 286720 | tf_op jit(solution)/shard_map/all_gather | solution.py:71
  42.2 0.6 convolution_convert_fusion
  42.8 1.4 copy.45
  44.2 0.0 all-to-all-done
  44.2 4.3 %all-to-all-start.1 = ((bf16[4,8,8,3584]{3,2,0,1:T(8,128)(2,1)}), bf16[4,8,8,3584]{3,2,0,1:T(8,128)(2,1)}, u32[]{:S(2)}, u32[]{:S(2)}) async-start(bf16[4,8,8,3584]{3,2,0,1:T(8,128)(2,1)} %copy.45), calls=%async_computation.1 | async-start | bytes 3670016 | tf_op jit(solution)/shard_map/all_to_all | solution.py:90
  48.5 0.0 reduce-scatter.2.cloned.1.call-start
  48.6 0.1 reshape.107
  48.7 0.2 copy.47
  48.8 0.1 reshape.99
  49.0 0.2 copy.49
  49.2 0.1 convert_reduce_fusion
  49.3 0.1 mul.20
  49.4 22.9 %all-to-all-done.1 = bf16[4,8,8,3584]{3,2,0,1:T(8,128)(2,1)} async-done(((bf16[4,8,8,3584]{3,2,0,1:T(8,128)(2,1)}), bf16[4,8,8,3584]{3,2,0,1:T(8,128)(2,1)}, u32[]{:S(2)}, u32[]{:S(2)}) %all-to-all-start.1) | async-done | bytes 1835040 | tf_op jit(solution)/shard_map/all_to_all | solution.py:90
  72.3 1.6 %copy.46 = bf16[4,8,8,3584]{3,2,1,0:T(8,128)(2,1)S(1)} copy(bf16[4,8,8,3584]{3,2,0,1:T(8,128)(2,1)} %all-to-all-done.1) | data formatting | bytes 3670016 | tf_op jit(solution)/shard_map/all_to_all | solution.py:90
  74.0 7.1 %fusion.5 = bf16[2,256,3584]{2,1,0:T(8,128)(2,1)} fusion(bf16[1,2,256,3584]{3,2,1,0:T(8,128)(2,1)} %param.19, bf16[256,3584,1]{1,0,2:T(8,128)(2,1)S(1)} %bitcast.66, bf16[1,2,3584,256]{3,2,1,0:T(8,128)(2,1)} %param.18), kind=kOutput, calls=%fused_computation.8 | convolution fusion | flops 1879179264 | bytes 12845056 | tf_op jit(solution)/shard_map/jnr,jrd->jnd/dot_general | solution.py:44
  81.1 0.0 copy-start
  81.1 14.9 %fusion = f32[256,1,3584]{2,1,0:T(1,128)} fusion(bf16[256,2,1]{1,2,0:T(2,128)(2,1)S(1)} %copy.49, bf16[2,256,3584]{2,1,0:T(8,128)(2,1)} %fusion.5), kind=kOutput, calls=%fused_computation | convolution fusion | flops 3670016 | bytes 7341056 | tf_op jit(solution)/shard_map/nj,jnd->nd/dot_general | solution.py:45
  96.0 0.0 copy-done
  96.0 1.1 fusion.12
  97.1 7.6 %fusion.3 = bf16[256,3584]{1,0:T(8,128)(2,1)} fusion(bf16[1,512,3584]{2,1,0:T(8,128)(2,1)} %param.17, f32[256,1,3584]{2,1,0:T(1,128)} %fusion, f32[256]{0:T(256)S(1)} %mul.20, bf16[256,3584]{1,0:T(8,128)(2,1)S(1)} %bitcast.68, bf16[1,3584,512]{2,1,0:T(8,128)(2,1)} %param.16, f32[256,512]{1,0:T(8,128)S(1)} %fusion.12), kind=kOutput, calls=%fused_computation.4 | convolution fusion | flops 1882587136 | bytes 15205376 | tf_op jit(solution)/shard_map/dot_general | solution.py:38
  104.7 0.0 reduce-scatter.2.cloned.1.call-update
  104.8 0.1 reduce_sum.49
  104.8 0.3 convert_reduce_fusion.2
  105.1 37.3 %reduce-scatter.2.cloned.1.call-done = bf16[64,3584]{1,0:T(8,128)(2,1)} async-done(((bf16[256,3584]{1,0:T(8,128)(2,1)}), bf16[64,3584]{1,0:T(8,128)(2,1)}) %reduce-scatter.2.cloned.1.call-update) | async-done | bytes 458768 | tf_op jit(solution)/shard_map/reduce_scatter | solution.py:102
  142.4 3.6 %all-to-all-start.2 = ((bf16[8,8,3584]{2,1,0:T(8,128)(2,1)}), bf16[8,8,3584]{2,1,0:T(8,128)(2,1)S(1)}, u32[]{:S(2)}, u32[]{:S(2)}) async-start(bf16[8,8,3584]{2,1,0:T(8,128)(2,1)} %bitcast.70), calls=%async_computation.3 | async-start | bytes 917504 | tf_op jit(solution)/shard_map/all_to_all | solution.py:110
  146.1 0.1 copy.40
  146.2 8.9 %all-to-all-done.2 = bf16[8,8,3584]{2,1,0:T(8,128)(2,1)S(1)} async-done(((bf16[8,8,3584]{2,1,0:T(8,128)(2,1)}), bf16[8,8,3584]{2,1,0:T(8,128)(2,1)S(1)}, u32[]{:S(2)}, u32[]{:S(2)}) %all-to-all-start.2) | async-done | bytes 458784 | tf_op jit(solution)/shard_map/all_to_all | solution.py:110
  155.0 1.0 fusion.4
  (10 shorter events, 0.1 us)
Async XLA Ops:
  24.4 19.8 %all-to-all-start = ((bf16[8,2,128]{2,1,0:T(2,128)(2,1)}), bf16[8,2,128]{2,1,0:T(2,128)(2,1)S(1)}, u32[]{:S(2)}, u32[]{:S(2)}) async-start(bf16[8,2,128]{2,1,0:T(2,128)(2,1)} %reshape.106), calls=%async_computation | async-start | bytes 8192 | tf_op jit(solution)/shard_map/all_to_all | solution.py:91
  44.2 28.1 %all-to-all-start.1 = ((bf16[4,8,8,3584]{3,2,0,1:T(8,128)(2,1)}), bf16[4,8,8,3584]{3,2,0,1:T(8,128)(2,1)}, u32[]{:S(2)}, u32[]{:S(2)}) async-start(bf16[4,8,8,3584]{3,2,0,1:T(8,128)(2,1)} %copy.45), calls=%async_computation.1 | async-start | bytes 3670016 | tf_op jit(solution)/shard_map/all_to_all | solution.py:90
  48.5 93.9 %reduce-scatter.2.cloned.1.call-start = ((), (), s32[]{:S(2)}) async-start(), calls=%async_computation.4 | async-start | bytes 2293760 | tf_op jit(solution)/shard_map/reduce_scatter | solution.py:102
  81.1 14.9 %copy-start = (bf16[1,3584,512]{2,1,0:T(8,128)(2,1)S(1)}, bf16[1,3584,512]{2,1,0:T(8,128)(2,1)}, u32[]{:S(2)}) copy-start(bf16[1,3584,512]{2,1,0:T(8,128)(2,1)} %param.15) | copy-start | bytes 11010052
  142.4 12.6 %all-to-all-start.2 = ((bf16[8,8,3584]{2,1,0:T(8,128)(2,1)}), bf16[8,8,3584]{2,1,0:T(8,128)(2,1)S(1)}, u32[]{:S(2)}, u32[]{:S(2)}) async-start(bf16[8,8,3584]{2,1,0:T(8,128)(2,1)} %bitcast.70), calls=%async_computation.3 | async-start | bytes 917504 | tf_op jit(solution)/shard_map/all_to_all | solution.py:110
Sparse Core Ops, SparseCore 0:
  104.9 37.4 reduce-scatter.1
where the time goes:
time: 163 us
  waiting for transfers between devices  69.1 us (42%)
  matrix products  32.6 us (20%)
  blocking collectives  27.7 us (17%)
  between operations  14.2 us (9%)
  starting transfers between devices  11.7 us (7%)
  local copies, waits for them, and re-layouts  4.78 us (3%)
  other arithmetic  2.95 us (2%)
    reduce_scatter x1, waiting for transfers between devices, body(): lax.psum_scatter(slice_term(flat_rows, flat_gates, gate_part, up_part, do...  37.3 us
    all_to_all x1, waiting for transfers between devices, body(): lax.all_to_all(sent_rows, 'expert', split_axis=1, concat_axis=1, tiled=True)  22.9 us
    dot_general x1, matrix products, slice_term(): deltas = jnp.einsum('nj,jnd->nd', own_gates, lifted)  14.9 us
    all_gather x1, blocking collectives, body(): lax.all_gather(tokens, 'dp', axis=0, tiled=True)  14 us
    all_gather x1, blocking collectives, body(): lax.all_gather(slot_gates, 'dp', axis=0, tiled=True)  13.6 us
    all_to_all x1, waiting for transfers between devices, body(): lax.all_to_all(summed.reshape(expert_size, capacity, width), 'expert', sp...  8.9 us
    dot_general x1, matrix products, slice_term(): shared = jnp.dot(hidden, down_part, preferred_element_type=jnp.float32)  7.62 us
    dot_general x1, matrix products, slice_term(): jnp.einsum('jnr,jrd->jnd', latent, out_part, preferred_element_type=jnp.f...  7.14 us
  transfers between devices with their start and end apart: 4, of which 3 were waited for; matrix products, arithmetic and copies ran while one was open for 2% of the time, Pallas kernels for 0%

commit v1 on v0

--- a/solution.py
+++ b/solution.py
@@ -5,6 +5,10 @@
 
 JSLOT = 8
 BTOP = 4
+meet_marks_up = lambda packet: jnp.concatenate(
+    lax.all_to_all(jnp.stack(jnp.split(packet, lax.axis_size("expert"), axis=1)), "expert", 0, 0),
+    axis=1,
+)
 
 
 def slot_table(routes, gate_values, expert_map, live_mask):
@@ -87,7 +91,7 @@
         preferred_element_type=jnp.float32,
     ).astype(jnp.bfloat16)
     got_rows, got_gates = (
-        lax.all_to_all(sent_rows, "expert", split_axis=1, concat_axis=1, tiled=True),
+        meet_marks_up(sent_rows),
         lax.all_to_all(sent_gates, "expert", split_axis=1, concat_axis=1, tiled=True),
     )
     flat_rows = got_rows.reshape(-1, width)

time: 163 us -> 164 us (level)
    unnamed x4 -> x15, local copies, waits for them, and re-layouts: 0.83 us -> 3.45 us
  transfers between devices with their start and end apart: 4 -> 4, of which waited for: 3 -> 3; matrix products, arithmetic and copies ran while one was open for 2% -> 1% of each run, Pallas kernels for 0% -> 0%
where the time goes in v1:
time: 164 us
  waiting for transfers between devices  69.1 us (42%)
  matrix products  32.6 us (20%)
  blocking collectives  27.7 us (17%)
  between operations  14.2 us (9%)
  starting transfers between devices  11.5 us (7%)
  local copies, waits for them, and re-layouts  6.02 us (4%)
  other arithmetic  2.95 us (2%)
    reduce_scatter x1, waiting for transfers between devices, body(): lax.psum_scatter(slice_term(flat_rows, flat_gates, gate_part, up_part, do...  37.3 us
    all_to_all x1, waiting for transfers between devices, lax.all_to_all(jnp.stack(jnp.split(packet, lax.axis_size('expert'), axis=...  22.9 us
    dot_general x1, matrix products, slice_term(): deltas = jnp.einsum('nj,jnd->nd', own_gates, lifted)  14.9 us
    all_gather x1, blocking collectives, body(): lax.all_gather(tokens, 'dp', axis=0, tiled=True)  14 us
    all_gather x1, blocking collectives, body(): lax.all_gather(slot_gates, 'dp', axis=0, tiled=True)  13.6 us
    all_to_all x1, waiting for transfers between devices, body(): lax.all_to_all(summed.reshape(expert_size, capacity, width), 'expert', sp...  8.9 us
    dot_general x1, matrix products, slice_term(): shared = jnp.dot(hidden, down_part, preferred_element_type=jnp.float32)  7.62 us
    dot_general x1, matrix products, slice_term(): jnp.einsum('jnr,jrd->jnd', latent, out_part, preferred_element_type=jnp.f...  7.14 us
  transfers between devices with their start and end apart: 4, of which 3 were waited for; matrix products, arithmetic and copies ran while one was open for 1% of the time, Pallas kernels for 0%

profile of v1, /device:TPU:0, one launch (start us, length us, event | category | flops | bytes accessed | tf_op | source)
XLA Modules:
  0.0 164.0 jit_solution(5512356673351259789)
XLA Ops:
  6.5 0.7 convert_element_type.85
  7.9 1.0 select_reduce_fusion.1
  8.9 0.1 select_reduce_fusion
  9.0 0.1 select_convert_fusion.1
  9.0 13.6 %all_gather.6 = bf16[32,64]{1,0:T(8,128)(2,1)S(1)} all-gather(bf16[8,64]{1,0:T(8,128)(2,1)S(1)} %select_convert_fusion.1), channel_id=1, replica_groups=mesh['dp'=4,'expert'=8] {'dp'}, dimensions={0}, use_global_device_ids=true | all-gather | bytes 5120 | tf_op jit(solution)/shard_map/all_gather | solution.py:76
  22.7 0.1 reshape_reshape.6
  22.8 0.6 convert_reduce_fusion.1
  23.5 0.1 copy.80
  23.5 0.2 convolution_convert_fusion.1
  23.7 0.7 reshape.106
  24.4 3.7 %all-to-all-start = ((bf16[8,2,128]{2,1,0:T(2,128)(2,1)}), bf16[8,2,128]{2,1,0:T(2,128)(2,1)S(1)}, u32[]{:S(2)}, u32[]{:S(2)}) async-start(bf16[8,2,128]{2,1,0:T(2,128)(2,1)} %reshape.106), calls=%async_computation | async-start | bytes 8192 | tf_op jit(solution)/shard_map/all_to_all | solution.py:95
  28.1 14.0 %all_gather.7 = bf16[32,3584]{1,0:T(8,128)(2,1)S(1)} all-gather(bf16[8,3584]{1,0:T(8,128)(2,1)} %param.10), channel_id=1, replica_groups=mesh['dp'=4,'expert'=8] {'dp'}, dimensions={0}, use_global_device_ids=true | all-gather | bytes 286720 | tf_op jit(solution)/shard_map/all_gather | solution.py:75
  42.2 0.6 convolution_convert_fusion
  43.0 0.0 copy-start.1
  43.0 1.2 copy-done.1
  44.2 0.0 all-to-all-done
  44.3 4.0 %all-to-all-start.1 = ((bf16[8,4,1,8,3584]{4,3,1,2,0:T(8,128)(2,1)}), bf16[8,4,1,8,3584]{4,3,1,2,0:T(8,128)(2,1)S(1)}, u32[]{:S(2)}, u32[]{:S(2)}) async-start(bf16[8,4,1,8,3584]{4,3,1,2,0:T(8,128)(2,1)} %copy-done.1), calls=%async_computation.1 | async-start | bytes 3670016 | tf_op jit(solution)/shard_map/all_to_all | solution.py:9
  48.3 0.0 reduce-scatter.2.cloned.1.call-start
  48.4 0.1 reshape.107
  48.5 0.2 copy.92
  48.6 0.1 reshape.99
  48.8 0.2 copy.94
  49.0 0.1 convert_reduce_fusion
  49.1 0.1 mul.20
  49.2 22.9 %all-to-all-done.1 = bf16[8,4,1,8,3584]{4,3,1,2,0:T(8,128)(2,1)S(1)} async-done(((bf16[8,4,1,8,3584]{4,3,1,2,0:T(8,128)(2,1)}), bf16[8,4,1,8,3584]{4,3,1,2,0:T(8,128)(2,1)S(1)}, u32[]{:S(2)}, u32[]{:S(2)}) %all-to-all-start.1) | async-done | bytes 1835040 | tf_op jit(solution)/shard_map/all_to_all | solution.py:9
  72.1 0.0 copy-start
  72.1 1.3 copy-done
  73.4 1.6 copy.91
  75.0 7.1 %fusion.5 = bf16[2,256,3584]{2,1,0:T(8,128)(2,1)} fusion(bf16[1,2,256,3584]{3,2,1,0:T(8,128)(2,1)} %param.19, bf16[256,3584,1]{1,0,2:T(8,128)(2,1)S(1)} %bitcast.113, bf16[1,2,3584,256]{3,2,1,0:T(8,128)(2,1)} %param.18), kind=kOutput, calls=%fused_computation.8 | convolution fusion | flops 1879179264 | bytes 12845056 | tf_op jit(solution)/shard_map/jnr,jrd->jnd/dot_general | solution.py:48
  82.1 0.0 copy-start.2
  82.2 14.9 %fusion = f32[256,1,3584]{2,1,0:T(1,128)} fusion(bf16[256,2,1]{1,2,0:T(2,128)(2,1)S(1)} %copy.94, bf16[2,256,3584]{2,1,0:T(8,128)(2,1)} %fusion.5), kind=kOutput, calls=%fused_computation | convolution fusion | flops 3670016 | bytes 7341056 | tf_op jit(solution)/shard_map/nj,jnd->nd/dot_general | solution.py:49
  97.0 0.0 copy-done.2
  97.0 1.1 fusion.12
  98.2 7.6 %fusion.3 = bf16[256,3584]{1,0:T(8,128)(2,1)} fusion(bf16[1,512,3584]{2,1,0:T(8,128)(2,1)} %param.17, f32[256,1,3584]{2,1,0:T(1,128)} %fusion, f32[256]{0:T(256)S(1)} %mul.20, bf16[256,3584]{1,0:T(8,128)(2,1)S(1)} %bitcast.115, bf16[1,3584,512]{2,1,0:T(8,128)(2,1)} %param.16, f32[256,512]{1,0:T(8,128)S(1)} %fusion.12), kind=kOutput, calls=%fused_computation.4 | convolution fusion | flops 1882587136 | bytes 15205376 | tf_op jit(solution)/shard_map/dot_general | solution.py:42
  105.8 0.0 reduce-scatter.2.cloned.1.call-update
  105.8 0.1 reduce_sum.49
  105.9 0.3 convert_reduce_fusion.2
  106.2 37.3 %reduce-scatter.2.cloned.1.call-done = bf16[64,3584]{1,0:T(8,128)(2,1)} async-done(((bf16[256,3584]{1,0:T(8,128)(2,1)}), bf16[64,3584]{1,0:T(8,128)(2,1)}) %reduce-scatter.2.cloned.1.call-update) | async-done | bytes 458768 | tf_op jit(solution)/shard_map/reduce_scatter | solution.py:106
  143.5 3.7 %all-to-all-start.2 = ((bf16[8,8,3584]{2,1,0:T(8,128)(2,1)}), bf16[8,8,3584]{2,1,0:T(8,128)(2,1)S(1)}, u32[]{:S(2)}, u32[]{:S(2)}) async-start(bf16[8,8,3584]{2,1,0:T(8,128)(2,1)} %bitcast.118), calls=%async_computation.3 | async-start | bytes 917504 | tf_op jit(solution)/shard_map/all_to_all | solution.py:114
  147.2 0.1 copy.79
  147.3 8.9 %all-to-all-done.2 = bf16[8,8,3584]{2,1,0:T(8,128)(2,1)S(1)} async-done(((bf16[8,8,3584]{2,1,0:T(8,128)(2,1)}), bf16[8,8,3584]{2,1,0:T(8,128)(2,1)S(1)}, u32[]{:S(2)}, u32[]{:S(2)}) %all-to-all-start.2) | async-done | bytes 458784 | tf_op jit(solution)/shard_map/all_to_all | solution.py:114
  156.1 1.0 fusion.4
  (18 shorter events, 0.2 us)
Async XLA Ops:
  24.4 19.8 %all-to-all-start = ((bf16[8,2,128]{2,1,0:T(2,128)(2,1)}), bf16[8,2,128]{2,1,0:T(2,128)(2,1)S(1)}, u32[]{:S(2)}, u32[]{:S(2)}) async-start(bf16[8,2,128]{2,1,0:T(2,128)(2,1)} %reshape.106), calls=%async_computation | async-start | bytes 8192 | tf_op jit(solution)/shard_map/all_to_all | solution.py:95
  43.0 1.3 copy-start.1
  44.3 27.9 %all-to-all-start.1 = ((bf16[8,4,1,8,3584]{4,3,1,2,0:T(8,128)(2,1)}), bf16[8,4,1,8,3584]{4,3,1,2,0:T(8,128)(2,1)S(1)}, u32[]{:S(2)}, u32[]{:S(2)}) async-start(bf16[8,4,1,8,3584]{4,3,1,2,0:T(8,128)(2,1)} %copy-done.1), calls=%async_computation.1 | async-start | bytes 3670016 | tf_op jit(solution)/shard_map/all_to_all | solution.py:9
  48.3 95.2 %reduce-scatter.2.cloned.1.call-start = ((), (), s32[]{:S(2)}) async-start(), calls=%async_computation.4 | async-start | bytes 2293760 | tf_op jit(solution)/shard_map/reduce_scatter | solution.py:106
  72.1 1.3 copy-start
  82.1 14.9 %copy-start.2 = (bf16[1,3584,512]{2,1,0:T(8,128)(2,1)S(1)}, bf16[1,3584,512]{2,1,0:T(8,128)(2,1)}, u32[]{:S(2)}) copy-start(bf16[1,3584,512]{2,1,0:T(8,128)(2,1)} %param.15) | copy-start | bytes 11010052
  143.5 12.7 %all-to-all-start.2 = ((bf16[8,8,3584]{2,1,0:T(8,128)(2,1)}), bf16[8,8,3584]{2,1,0:T(8,128)(2,1)S(1)}, u32[]{:S(2)}, u32[]{:S(2)}) async-start(bf16[8,8,3584]{2,1,0:T(8,128)(2,1)} %bitcast.118), calls=%async_computation.3 | async-start | bytes 917504 | tf_op jit(solution)/shard_map/all_to_all | solution.py:114
Sparse Core Ops, SparseCore 0:
  105.9 37.5 reduce-scatter.1
